TPU v7x, 32 devices: a whole 2x2x4 slice. The times are simulated.
32 devices in a mesh: mz: 8 (over z, x), rep: 4 (over y, core).
Axes of the slice: x: 2, y: 2, z: 4, core: 2. Of those that a mesh axis runs over, the one named last changes fastest.
Arguments:
- spectra: bfloat16 [131072, 512], P(('mz', 'rep')), may hold values from -6 to 6
- reach_back: int32 [131072], P(('mz', 'rep')), may hold values from 0 to 256
- reach_ahead: int32 [131072], P(('mz', 'rep')), may hold values from 0 to 256
- live: int32 [32], P(('mz', 'rep')), may hold values from 1024 to 4096, as said below
- cluster_ids: int32 [131072], P(('mz', 'rep')), may hold values from 0 to 16383, as said below
Outputs:
- cluster_vectors: float32 [16384, 512], P(('mz', 'rep'))
Inputs may be any that keep to these rules, and one draw needn't show every extreme that they name: Device d holds slots d * 4096 to (d + 1) * 4096 - 1, of which the first live[d] are occupied; at least one device is full. `cluster_ids`: cluster k is owned by m/z range k div (512 * 4). Range d is held by devices d * 4 to d * 4 + 4 - 1 in order of rising m/z; a spectrum on the first of them belongs to a cluster owned by range d - 1 or d, one on the last of them to a cluster owned by range d or d + 1, and one on any other to a cluster owned by range d.
All inputs are finite; a program needn't handle non-finite values.
Results may differ from a plain program's by a relative error of at most 0.0046.
Values may be sent and summed in bfloat16 or wider, within the bound.
A program may use at most 128 MiB of HBM per device.

v0:
```python
import jax
import jax.numpy as jnp
from jax import lax
from jax.sharding import PartitionSpec as P

DIM = 512
BLOCK = 256
CL_DEV = 512


sharpness = 3.0


def extended(block, sides, width):
    for axis, dim in sides:
        count = lax.axis_size(axis)
        forward = [(i, i + 1) for i in range(count - 1)]
        backward = [(target, source) for source, target in forward]
        low = lax.ppermute(
            lax.slice_in_dim(block, block.shape[dim] - width, None, axis=dim), axis, forward
        )
        high = lax.ppermute(lax.slice_in_dim(block, 0, width, axis=dim), axis, backward)
        block = jnp.concatenate([low, block, high], axis=dim)
    return block


def shifted(block, axis, distance):
    devices = range(lax.axis_size(axis))
    route = [(i - distance, i) for i in devices if i - distance in devices]
    return lax.ppermute(block, axis, route)


def rows_block(queries, query_pos, back, ahead, keys, key_flags, key_start):
    scores = lax.dot_general(
        queries, keys, (((1,), (1,)), ((), ())), preferred_element_type=jnp.float32
    )
    key_pos = key_start + jnp.arange(keys.shape[0], dtype=jnp.int32)
    offset = key_pos[None, :] - query_pos[:, None]
    inside = (offset >= -back[:, None]) & (offset <= ahead[:, None]) & (key_flags[None, :] > 0)
    keep = inside | (offset == 0)
    weight = jnp.where(keep, jnp.exp(sharpness * (scores - 1.0)), jnp.float32(0.0))
    total = jnp.sum(weight, axis=1, keepdims=True)
    mixed = jnp.dot(weight.astype(jnp.bfloat16), keys, preferred_element_type=jnp.float32)
    return (mixed / total).astype(jnp.bfloat16)


def shards(spectra, reach_back, reach_ahead, live, cluster_ids):
    rows = spectra.shape[0]
    values = spectra.astype(jnp.float32)
    unit = (values / jnp.sqrt(jnp.sum(values * values, axis=1, keepdims=True) + 1e-06)).astype(
        jnp.bfloat16
    )
    present = jnp.arange(rows, dtype=jnp.int32) < live[0]
    flags = present.astype(jnp.bfloat16)
    wide_unit, wide_flags = (
        extended(unit, ((("mz", "rep"), 0),), BLOCK),
        extended(flags, ((("mz", "rep"), 0),), BLOCK),
    )
    pieces = []
    for index in range(rows // BLOCK):
        start = index * BLOCK
        query_pos = start + jnp.arange(BLOCK, dtype=jnp.int32)
        pieces.append(
            rows_block(
                unit[start : start + BLOCK],
                query_pos,
                reach_back[start : start + BLOCK],
                reach_ahead[start : start + BLOCK],
                wide_unit[start : start + 3 * BLOCK],
                wide_flags[start : start + 3 * BLOCK],
                start - BLOCK,
            )
        )
    consensus = jnp.concatenate(pieces, axis=0)
    kept = consensus.astype(jnp.float32) * present.astype(jnp.float32)[:, None]
    rep_count = lax.axis_size("rep")
    per_range = CL_DEV * rep_count
    local_slot = cluster_ids - (lax.axis_index("mz") - 1) * per_range
    partial_value = jax.ops.segment_sum(kept, local_slot, num_segments=3 * per_range).reshape(
        3, per_range, DIM
    )
    edge_part = jnp.where(lax.axis_index("rep") == 0, partial_value[0], partial_value[2])
    stacked = jnp.stack([partial_value[1], edge_part]).reshape(2, rep_count, CL_DEV, DIM)
    arrived = lax.all_to_all(stacked, "rep", split_axis=1, concat_axis=1, tiled=True)
    own_sum = jnp.sum(arrived[0], axis=0)
    from_above = shifted(arrived[1, 0].astype(jnp.bfloat16), "mz", -1).astype(jnp.float32)
    from_below = shifted(arrived[1, rep_count - 1].astype(jnp.bfloat16), "mz", 1).astype(
        jnp.float32
    )
    owned = own_sum + from_below + from_above
    scale = jnp.sqrt(jnp.mean(owned * owned, axis=1, keepdims=True) + 1e-06)
    return owned / scale


def solution(mesh):
    return jax.shard_map(
        shards,
        mesh=mesh,
        in_specs=(
            P(("mz", "rep"), None),
            P(("mz", "rep")),
            P(("mz", "rep")),
            P(("mz", "rep")),
            P(("mz", "rep")),
        ),
        out_specs=P(("mz", "rep"), None),
        check_vma=False,
    )
```

profile of v0, /device:TPU:3, one launch (start us, length us, event | category | flops | bytes accessed | tf_op | source)
XLA Modules:
  0.0 219.0 jit_solution(7873283192365824789)
XLA Ops:
  0.8 2.7 %collective-permute-start.2 = (bf16[256]{0:T(256)(128)(2,1)S(1)}, bf16[256]{0:T(256)(128)(2,1)S(1)}, u32[]{:S(2)}, u32[]{:S(2)}) collective-permute-start(bf16[256]{0:T(256)(128)(2,1)S(1)} %get-tuple-element.61), channel_id=1, source_target_pairs={{1,0},{2,1},{3,2},{4,3},{5,4},{6,5},{7,6},{8,7},{9,8},{10,9},{11,1... | collective-permute-start | bytes 1544 | tf_op jit(solution)/shard_map/ppermute | solution.py:22
  3.6 3.0 %collective-permute-start = (bf16[256]{0:T(256)(128)(2,1)S(1)}, bf16[256]{0:T(256)(128)(2,1)S(1)}, u32[]{:S(2)}, u32[]{:S(2)}) collective-permute-start(bf16[256]{0:T(256)(128)(2,1)S(1)} %get-tuple-element.62), channel_id=1, source_target_pairs={{0,1},{1,2},{2,3},{3,4},{4,5},{5,6},{6,7},{7,8},{8,9},{9,10},{10,1... | collective-permute-start | bytes 1544 | tf_op jit(solution)/shard_map/ppermute | solution.py:19
  6.6 3.1 %fusion = f32[4096]{0:T(1024)S(1)} fusion(bf16[4096,512]{1,0:T(8,128)(2,1)} %param.5), kind=kLoop, calls=%fused_computation.3 | loop fusion | flops 6287360 | bytes 4210688 | tf_op jit(solution)/shard_map/reduce_sum | solution.py:50
  9.8 1.0 fusion.1
  10.8 1.9 copy-done
  12.8 1.9 collective-permute-start.3
  14.7 3.6 %collective-permute-start.1 = (bf16[256,512]{1,0:T(8,128)(2,1)S(1)}, bf16[256,512]{1,0:T(8,128)(2,1)S(1)}, u32[]{:S(2)}, u32[]{:S(2)}) collective-permute-start(bf16[256,512]{1,0:T(8,128)(2,1)S(1)} %get-tuple-element.12), channel_id=1, source_target_pairs={{0,1},{1,2},{2,3},{3,4},{4,5},{5,6},{6,7},{7,8},{8,9},{9,10},{10,1... | collective-permute-start | bytes 786440 | tf_op jit(solution)/shard_map/ppermute | solution.py:19
  18.8 2.0 fusion.223
  30.7 1.1 fusion.56
  31.8 1.1 fusion.58
  32.9 1.1 fusion.60
  34.0 1.1 fusion.62
  35.1 1.1 fusion.64
  36.1 1.1 fusion.66
  37.2 1.1 fusion.68
  38.3 1.1 fusion.70
  39.3 1.1 fusion.72
  40.4 1.1 fusion.74
  41.5 1.1 fusion.76
  42.6 1.1 fusion.78
  43.7 1.2 fusion.80
  44.9 1.1 fusion.82
  46.0 1.1 fusion.84
  47.7 1.1 fusion.86
  48.8 32.5 %scatter_custom_fusion = f32[6144,512]{1,0:T(8,128)} fusion(s32[4096]{0:T(1024)S(1)} %broadcast_subtract_fusion, bf16[4096,512]{1,0:T(8,128)(2,1)} %fusion.86, f32[]{:T(128)} %constant.27.clone.1, f32[4096]{0:T(1024)S(1)} %get-tuple-element.95), kind=kCustom, calls=%fused_computation.6 | custom fusion | flops 6291456 | bytes 16793604 | tf_op jit(solution)/shard_map/scatter-add | solution.py:79
  81.3 8.2 %fusion.205 = (f32[2048,512]{1,0:T(8,128)S(1)}, f32[2048,512]{1,0:T(8,128)}) fusion(f32[6144,512]{1,0:T(8,128)} %scatter_custom_fusion, pred[]{:T(512)S(6)} %eq.67), kind=kLoop, calls=%fused_computation.360 | loop fusion | flops 1048576 | bytes 20971520 | tf_op jit(solution)/shard_map/slice | solution.py:83
  89.5 3.6 %pad_maximum_fusion = f32[2,4,512,512]{3,2,0,1:T(8,128)S(1)} fusion(f32[1,4,512,512]{3,2,0,1:T(8,128)} %bitcast.31, f32[1,4,512,512]{3,2,0,1:T(8,128)S(1)} %bitcast.30), kind=kLoop, calls=%fused_computation.5 | loop fusion | flops 2097152 | bytes 16777216 | tf_op jit(solution)/shard_map/stack | solution.py:83
  93.1 98.3 %all_to_all.5 = f32[2,4,512,512]{3,2,0,1:T(8,128)S(1)} all-to-all(f32[2,4,512,512]{3,2,0,1:T(8,128)S(1)} %pad_maximum_fusion), channel_id=1, replica_groups=mesh['mz'=8,'rep'=4] {'rep'}, dimensions={1} | all-to-all | bytes 16777216 | tf_op jit(solution)/shard_map/all_to_all | solution.py:84
  192.0 2.1 collective-permute-start.4
  194.1 3.2 %collective-permute-start.5 = (bf16[512,512]{1,0:T(8,128)(2,1)S(1)}, bf16[512,512]{1,0:T(8,128)(2,1)S(1)}, u32[]{:S(2)}, u32[]{:S(2)}) collective-permute-start(bf16[512,512]{1,0:T(8,128)(2,1)S(1)} %get-tuple-element.8), channel_id=1, source_target_pairs={{4,0},{8,4},{12,8},{16,12},{20,16},{24,20},{28,24},{5,1},{9,5},{13... | collective-permute-start | bytes 1572872 | tf_op jit(solution)/shard_map/ppermute | solution.py:30
  197.9 19.7 %collective-permute-done.4 = bf16[512,512]{1,0:T(8,128)(2,1)S(1)} collective-permute-done((bf16[512,512]{1,0:T(8,128)(2,1)S(1)}, bf16[512,512]{1,0:T(8,128)(2,1)S(1)}, u32[]{:S(2)}, u32[]{:S(2)}) %collective-permute-start.4) | collective-permute-done | bytes 524320 | tf_op jit(solution)/shard_map/ppermute | solution.py:30
  217.9 1.2 broadcast_divide_fusion
  (74 shorter events, 12.2 us)
Async XLA Ops:
  0.0 9.7 %copy-start.2 = (bf16[4096,512]{1,0:T(8,128)(2,1)S(1)}, bf16[4096,512]{1,0:T(8,128)(2,1)}, u32[]{:S(2)}) copy-start(bf16[4096,512]{1,0:T(8,128)(2,1)} %param.5) | copy-start | bytes 12582916
  0.8 17.9 %collective-permute-start.2 = (bf16[256]{0:T(256)(128)(2,1)S(1)}, bf16[256]{0:T(256)(128)(2,1)S(1)}, u32[]{:S(2)}, u32[]{:S(2)}) collective-permute-start(bf16[256]{0:T(256)(128)(2,1)S(1)} %get-tuple-element.61), channel_id=1, source_target_pairs={{1,0},{2,1},{3,2},{4,3},{5,4},{6,5},{7,6},{8,7},{9,8},{10,9},{11,1... | collective-permute-start | bytes 1544 | tf_op jit(solution)/shard_map/ppermute | solution.py:22
  3.6 15.2 %collective-permute-start = (bf16[256]{0:T(256)(128)(2,1)S(1)}, bf16[256]{0:T(256)(128)(2,1)S(1)}, u32[]{:S(2)}, u32[]{:S(2)}) collective-permute-start(bf16[256]{0:T(256)(128)(2,1)S(1)} %get-tuple-element.62), channel_id=1, source_target_pairs={{0,1},{1,2},{2,3},{3,4},{4,5},{5,6},{6,7},{7,8},{8,9},{9,10},{10,1... | collective-permute-start | bytes 1544 | tf_op jit(solution)/shard_map/ppermute | solution.py:19
  9.7 8.9 %copy-start.3 = (s32[4096]{0:T(1024)S(1)}, s32[4096]{0:T(1024)}, u32[]{:S(2)}) copy-start(s32[4096]{0:T(1024)} %param.7) | copy-start | bytes 49156
  9.7 8.9 %copy-start.4 = (s32[4096]{0:T(1024)S(1)}, s32[4096]{0:T(1024)}, u32[]{:S(2)}) copy-start(s32[4096]{0:T(1024)} %param.6) | copy-start | bytes 49156
  9.7 9.0 %copy-start.5 = (s32[4096]{0:T(1024)S(1)}, s32[4096]{0:T(1024)}, u32[]{:S(2)}) copy-start(s32[4096]{0:T(1024)} %param.9) | copy-start | bytes 49156
  10.8 1.9 copy-start
  12.8 17.2 %collective-permute-start.3 = (bf16[256,512]{1,0:T(8,128)(2,1)S(1)}, bf16[256,512]{1,0:T(8,128)(2,1)S(1)}, u32[]{:S(2)}, u32[]{:S(2)}) collective-permute-start(bf16[256,512]{1,0:T(8,128)(2,1)S(1)} %get-tuple-element.11), channel_id=1, source_target_pairs={{1,0},{2,1},{3,2},{4,3},{5,4},{6,5},{7,6},{8,7},{9,8},{10,9},{11,1... | collective-permute-start | bytes 786440 | tf_op jit(solution)/shard_map/ppermute | solution.py:22
  14.7 15.2 %collective-permute-start.1 = (bf16[256,512]{1,0:T(8,128)(2,1)S(1)}, bf16[256,512]{1,0:T(8,128)(2,1)S(1)}, u32[]{:S(2)}, u32[]{:S(2)}) collective-permute-start(bf16[256,512]{1,0:T(8,128)(2,1)S(1)} %get-tuple-element.12), channel_id=1, source_target_pairs={{0,1},{1,2},{2,3},{3,4},{4,5},{5,6},{6,7},{7,8},{8,9},{9,10},{10,1... | collective-permute-start | bytes 786440 | tf_op jit(solution)/shard_map/ppermute | solution.py:19
  18.7 2.5 %copy-start.1 = (bf16[4096,512]{1,0:T(8,128)(2,1)S(1)}, bf16[4096,512]{1,0:T(8,128)(2,1)}, u32[]{:S(2)}) copy-start(bf16[4096,512]{1,0:T(8,128)(2,1)} %copy-done) | copy-start | bytes 12582916
  192.0 25.6 %collective-permute-start.4 = (bf16[512,512]{1,0:T(8,128)(2,1)S(1)}, bf16[512,512]{1,0:T(8,128)(2,1)S(1)}, u32[]{:S(2)}, u32[]{:S(2)}) collective-permute-start(bf16[512,512]{1,0:T(8,128)(2,1)S(1)} %get-tuple-element.7), channel_id=1, source_target_pairs={{0,4},{4,8},{8,12},{12,16},{16,20},{20,24},{24,28},{1,5},{5,9},{9,... | collective-permute-start | bytes 1572872 | tf_op jit(solution)/shard_map/ppermute | solution.py:30
  194.1 23.5 %collective-permute-start.5 = (bf16[512,512]{1,0:T(8,128)(2,1)S(1)}, bf16[512,512]{1,0:T(8,128)(2,1)S(1)}, u32[]{:S(2)}, u32[]{:S(2)}) collective-permute-start(bf16[512,512]{1,0:T(8,128)(2,1)S(1)} %get-tuple-element.8), channel_id=1, source_target_pairs={{4,0},{8,4},{12,8},{16,12},{20,16},{24,20},{28,24},{5,1},{9,5},{13... | collective-permute-start | bytes 1572872 | tf_op jit(solution)/shard_map/ppermute | solution.py:30
where the time goes:
time: 221 us; the launch traced here: 219 us
  blocking collectives  98.3 us (44%)
  other arithmetic  51.2 us (23%)
  matrix products  29.5 us (13%)
  waiting for transfers between devices  19.7 us (9%)
  starting transfers between devices  16.6 us (8%)
  local copies, waits for them, and re-layouts  2.48 us (1%)
    all_to_all x1, blocking collectives, shards(): lax.all_to_all(stacked, 'rep', split_axis=1, concat_axis=1, tiled=True)  98.3 us
    scatter-add x1, other arithmetic, shards(): jax.ops.segment_sum(kept, local_slot, num_segments=3 * per_range)  32.5 us
    ppermute x2, waiting for transfers between devices, shifted(): return lax.ppermute(block, axis, route)  19.7 us
    dot_general x16, matrix products, rows_block(): jnp.dot(weight.astype(jnp.bfloat16), keys, preferred_element_type=jnp.flo...  17.4 us
    dot_general x16, matrix products, rows_block(): lax.dot_general(queries, keys, (((1,), (1,)), ((), ())), preferred_elemen...  12.1 us
    slice x1, other arithmetic, shards(): partial_value[1]  8.16 us
    ppermute x2, starting transfers between devices, extended(): lax.ppermute(lax.slice_in_dim(block, block.shape[dim] - width, None, axis...  6.69 us
    ppermute x2, starting transfers between devices, shifted(): return lax.ppermute(block, axis, route)  5.31 us
  transfers between devices with their start and end apart: 6, of which 1 were waited for; matrix products, arithmetic and copies ran while one was open for 7% of the time, Pallas kernels for 0%

commit v1 on v0

--- a/solution.py
+++ b/solution.py
@@ -75,19 +75,25 @@
     kept = consensus.astype(jnp.float32) * present.astype(jnp.float32)[:, None]
     rep_count = lax.axis_size("rep")
     per_range = CL_DEV * rep_count
-    local_slot = cluster_ids - (lax.axis_index("mz") - 1) * per_range
-    partial_value = jax.ops.segment_sum(kept, local_slot, num_segments=3 * per_range).reshape(
-        3, per_range, DIM
-    )
-    edge_part = jnp.where(lax.axis_index("rep") == 0, partial_value[0], partial_value[2])
-    stacked = jnp.stack([partial_value[1], edge_part]).reshape(2, rep_count, CL_DEV, DIM)
-    arrived = lax.all_to_all(stacked, "rep", split_axis=1, concat_axis=1, tiled=True)
-    own_sum = jnp.sum(arrived[0], axis=0)
-    from_above = shifted(arrived[1, 0].astype(jnp.bfloat16), "mz", -1).astype(jnp.float32)
-    from_below = shifted(arrived[1, rep_count - 1].astype(jnp.bfloat16), "mz", 1).astype(
-        jnp.float32
-    )
-    owned = own_sum + from_below + from_above
+    span = 2 * per_range
+    local = cluster_ids - lax.axis_index("mz") * per_range
+    slot = jnp.where(local < 0, local + span, local)
+    partial_value = jax.ops.segment_sum(kept, slot, num_segments=span).astype(jnp.bfloat16)
+    parts = partial_value.reshape(2, rep_count, CL_DEV, DIM)
+    arrived = lax.all_to_all(parts[0], "rep", split_axis=0, concat_axis=0, tiled=True)
+    owned = jnp.sum(arrived.astype(jnp.float32), axis=0)
+    mz_count = lax.axis_size("mz")
+    first = lax.axis_index("rep") == 0
+    turn = rep_count // 2
+    for step in range(rep_count):
+        other = (step + turn) % rep_count
+        route = [(d * rep_count, (d - 1) * rep_count + step) for d in range(1, mz_count)]
+        route += [
+            (d * rep_count + rep_count - 1, (d + 1) * rep_count + other)
+            for d in range(mz_count - 1)
+        ]
+        piece = jnp.where(first, parts[1, step], parts[1, other])
+        owned = owned + lax.ppermute(piece, ("mz", "rep"), route).astype(jnp.float32)
     scale = jnp.sqrt(jnp.mean(owned * owned, axis=1, keepdims=True) + 1e-06)
     return owned / scale
 

time: 221 us -> 138 us (0.62)
  blocking collectives: 98.3 us -> 0 us
  waiting for transfers between devices: 19.7 us -> 31.9 us
  starting transfers between devices: 16.6 us -> 22.4 us
  other arithmetic: 51.2 us -> 46.7 us
  local copies, waits for them, and re-layouts: 2.48 us -> 5.56 us
    all_to_all x1 -> x0, blocking collectives: 98.3 us -> none  [shards(): lax.all_to_all(stacked, 'rep', split_axis=1, concat_axis=1, tiled=True)]
    all_to_all x0 -> x1, waiting for transfers between devices: none -> 29.4 us  [shards(): lax.all_to_all(parts[0], 'rep', split_axis=0, concat_axis=0, tiled=True)]
    ppermute x2 -> x4, waiting for transfers between devices: 19.7 us -> 0.01 us  [shards(): lax.ppermute(piece, ('mz', 'rep'), route).astype(jnp.float32)]
    slice x1 -> x0, other arithmetic: 8.16 us -> none  [shards(): partial_value[1]]
    all_to_all x0 -> x1, starting transfers between devices: none -> 6.47 us  [shards(): lax.all_to_all(parts[0], 'rep', split_axis=0, concat_axis=0, tiled=True)]
    another operation x2 -> x0, other arithmetic: 4.17 us -> none  [the longest x1 3.63 us: shards(): jnp.stack([partial_value[1], edge_part]).reshape(2, rep_count, CL_DEV, DIM)]
    convert_element_type x0 -> x1, other arithmetic: none -> 3.92 us  [shards(): jax.ops.segment_sum(kept, slot, num_segments=span).astype(jnp.bfloat16)]
    select_n x0 -> x2, other arithmetic: none -> 2.94 us  [the longest x1 2.94 us: shards(): piece = jnp.where(first, parts[1, step], parts[1, other])]
  transfers between devices with their start and end apart: 6 -> 9, of which waited for: 1 -> 2; matrix products, arithmetic and copies ran while one was open for 7% -> 10% of each run, Pallas kernels for 0% -> 0%
where the time goes in v1:
time: 138 us; the launch traced here: 137 us
  other arithmetic  46.7 us (34%)
  waiting for transfers between devices  31.9 us (23%)
  matrix products  29.4 us (21%)
  starting transfers between devices  22.4 us (16%)
  local copies, waits for them, and re-layouts  5.56 us (4%)
    scatter-add x1, other arithmetic, shards(): jax.ops.segment_sum(kept, slot, num_segments=span).astype(jnp.bfloat16)  30.8 us
    all_to_all x1, waiting for transfers between devices, shards(): lax.all_to_all(parts[0], 'rep', split_axis=0, concat_axis=0, tiled=True)  29.4 us
    dot_general x16, matrix products, rows_block(): jnp.dot(weight.astype(jnp.bfloat16), keys, preferred_element_type=jnp.flo...  17.5 us
    dot_general x16, matrix products, rows_block(): lax.dot_general(queries, keys, (((1,), (1,)), ((), ())), preferred_elemen...  11.9 us
    ppermute x2, starting transfers between devices, extended(): lax.ppermute(lax.slice_in_dim(block, block.shape[dim] - width, None, axis...  7.35 us
    all_to_all x1, starting transfers between devices, shards(): lax.all_to_all(parts[0], 'rep', split_axis=0, concat_axis=0, tiled=True)  6.47 us
    ppermute x4, starting transfers between devices, shards(): lax.ppermute(piece, ('mz', 'rep'), route).astype(jnp.float32)  4.73 us
    unnamed x14, local copies, waits for them, and re-layouts  4.04 us
  transfers between devices with their start and end apart: 9, of which 2 were waited for; matrix products, arithmetic and copies ran while one was open for 10% of the time, Pallas kernels for 0%

profile of v1, /device:TPU:3, one launch (start us, length us, event | category | flops | bytes accessed | tf_op | source)
XLA Modules:
  0.0 137.1 jit_solution(4667905118919874059)
XLA Ops:
  0.0 3.2 %fusion = f32[4096]{0:T(1024)S(1)} fusion(bf16[4096,512]{1,0:T(8,128)(2,1)} %param.5), kind=kLoop, calls=%fused_computation.3 | loop fusion | flops 6287360 | bytes 4210688 | tf_op jit(solution)/shard_map/reduce_sum | solution.py:50
  4.5 1.9 %copy-done = bf16[4096,512]{1,0:T(8,128)(2,1)} copy-done((bf16[4096,512]{1,0:T(8,128)(2,1)}, bf16[4096,512]{1,0:T(8,128)(2,1)S(1)}, u32[]{:S(2)}) %copy-start) | copy-done | bytes 4194328
  6.4 3.7 %collective-permute-start.1 = (bf16[256,512]{1,0:T(8,128)(2,1)S(1)}, bf16[256,512]{1,0:T(8,128)(2,1)S(1)}, u32[]{:S(2)}, u32[]{:S(2)}) collective-permute-start(bf16[256,512]{1,0:T(8,128)(2,1)S(1)} %get-tuple-element.12), channel_id=1, source_target_pairs={{0,1},{1,2},{2,3},{3,4},{4,5},{5,6},{6,7},{7,8},{8,9},{9,10},{10,1... | collective-permute-start | bytes 786440 | tf_op jit(solution)/shard_map/ppermute | solution.py:19
  10.2 1.9 %collective-permute-start.3 = (bf16[256,512]{1,0:T(8,128)(2,1)S(1)}, bf16[256,512]{1,0:T(8,128)(2,1)S(1)}, u32[]{:S(2)}, u32[]{:S(2)}) collective-permute-start(bf16[256,512]{1,0:T(8,128)(2,1)S(1)} %get-tuple-element.11), channel_id=1, source_target_pairs={{1,0},{2,1},{3,2},{4,3},{5,4},{6,5},{7,6},{8,7},{9,8},{10,9},{11,1... | collective-permute-start | bytes 786440 | tf_op jit(solution)/shard_map/ppermute | solution.py:22
  12.8 3.6 %collective-permute-start = (bf16[256]{0:T(256)(128)(2,1)S(1)}, bf16[256]{0:T(256)(128)(2,1)S(1)}, u32[]{:S(2)}, u32[]{:S(2)}) collective-permute-start(bf16[256]{0:T(256)(128)(2,1)S(1)} %get-tuple-element.62), channel_id=1, source_target_pairs={{0,1},{1,2},{2,3},{3,4},{4,5},{5,6},{6,7},{7,8},{8,9},{9,10},{10,1... | collective-permute-start | bytes 1544 | tf_op jit(solution)/shard_map/ppermute | solution.py:19
  16.4 1.9 %collective-permute-start.2 = (bf16[256]{0:T(256)(128)(2,1)S(1)}, bf16[256]{0:T(256)(128)(2,1)S(1)}, u32[]{:S(2)}, u32[]{:S(2)}) collective-permute-start(bf16[256]{0:T(256)(128)(2,1)S(1)} %get-tuple-element.61), channel_id=1, source_target_pairs={{1,0},{2,1},{3,2},{4,3},{5,4},{6,5},{7,6},{8,7},{9,8},{10,9},{11,1... | collective-permute-start | bytes 1544 | tf_op jit(solution)/shard_map/ppermute | solution.py:22
  18.8 2.5 %collective-permute-done.2 = bf16[256]{0:T(256)(128)(2,1)S(1)} collective-permute-done((bf16[256]{0:T(256)(128)(2,1)S(1)}, bf16[256]{0:T(256)(128)(2,1)S(1)}, u32[]{:S(2)}, u32[]{:S(2)}) %collective-permute-start.2) | collective-permute-done | bytes 544 | tf_op jit(solution)/shard_map/ppermute | solution.py:22
  21.3 1.9 %fusion.210 = (f32[256]{0:T(256)S(1)}, bf16[256,768]{1,0:T(8,128)(2,1)S(1)}) fusion(bf16[4096,512]{1,0:T(8,128)(2,1)} %copy-done, pred[768]{0:T(1024)(128)(4,1)S(1)} %get-tuple-element.59, s32[256]{0:T(256)S(1)} %get-tuple-element.41, s32[256]{0:T(256)S(1)} %get-tuple-element.25, s32[256]{0:T(256)S(1)} %iota_add_fusion.28, s32[768]{0:T(1024)S(1)} %iota_add_fusion.13), kind=kOutput, calls=%fused_computation.365 | convolution fusion | flops 203685632 | bytes 1449728 | tf_op jit(solution)/shard_map/dot_general | solution.py:34
  32.7 1.1 fusion.56
  34.9 1.1 fusion.60
  35.9 1.1 fusion.62
  37.0 1.1 fusion.64
  38.1 1.1 fusion.66
  39.2 1.1 fusion.68
  40.3 1.1 fusion.70
  41.4 1.1 fusion.72
  42.5 1.1 fusion.74
  43.6 1.1 fusion.76
  45.7 1.2 fusion.80
  49.7 1.1 fusion.86
  50.8 30.8 %scatter_custom_fusion = f32[4096,512]{1,0:T(8,128)} fusion(s32[4096]{0:T(1024)S(1)} %compare_select_fusion, bf16[4096,512]{1,0:T(8,128)(2,1)} %fusion.86, f32[4096]{0:T(1024)S(1)} %get-tuple-element.95, f32[]{:T(128)} %constant.27.clone.1), kind=kCustom, calls=%fused_computation.5 | custom fusion | flops 6291456 | bytes 12599300 | tf_op jit(solution)/shard_map/scatter-add | solution.py:81
  81.7 3.9 %convert_element_type.170 = bf16[4096,512]{1,0:T(8,128)(2,1)S(1)} convert(f32[4096,512]{1,0:T(8,128)} %scatter_custom_fusion) | non-fusion elementwise | flops 2097152 | bytes 12582912 | tf_op jit(solution)/shard_map/convert_element_type | solution.py:81
  85.6 1.9 %copy-done.2 = bf16[4096,512]{1,0:T(8,128)(2,1)} copy-done((bf16[4096,512]{1,0:T(8,128)(2,1)}, bf16[4096,512]{1,0:T(8,128)(2,1)S(1)}, u32[]{:S(2)}) %copy-start.2) | copy-done | bytes 4194328
  87.5 1.5 %slice.405 = bf16[2048,512]{1,0:T(8,128)(2,1)} slice(bf16[4096,512]{1,0:T(8,128)(2,1)S(1)} %convert_element_type.170), slice={[0:2048], [0:512]} | slice | bytes 4194304 | tf_op jit(solution)/shard_map/slice | solution.py:83
  89.0 6.5 %all-to-all-start = ((bf16[4,512,512]{2,1,0:T(8,128)(2,1)}), bf16[4,512,512]{2,1,0:T(8,128)(2,1)S(1)}, u32[]{:S(2)}, u32[]{:S(2)}) async-start(bf16[4,512,512]{2,1,0:T(8,128)(2,1)} %bitcast.33), calls=%async_computation | async-start | bytes 4194304 | tf_op jit(solution)/shard_map/all_to_all | solution.py:83
  95.5 2.9 %select_bitcast_fusion.3 = (bf16[512,512]{1,0:T(8,128)(2,1)}, bf16[512,512]{1,0:T(8,128)(2,1)}, bf16[512,512]{1,0:T(8,128)(2,1)}, bf16[512,512]{1,0:T(8,128)(2,1)}) fusion(pred[]{:T(512)S(6)} %eq.67, bf16[2,4,512,512]{3,2,1,0:T(8,128)(2,1)} %bitcast.32), kind=kLoop, calls=%fused_computation.257 | loop fusion | flops 1048576 | bytes 4194305 | tf_op jit(solution)/shard_map/jit(_where)/select_n | solution.py:95
  99.1 1.3 collective-permute-start.5
  100.4 1.5 %collective-permute-start.6 = (bf16[512,512]{1,0:T(8,128)(2,1)}, bf16[512,512]{1,0:T(8,128)(2,1)}, u32[]{:S(2)}, u32[]{:S(2)}) collective-permute-start(bf16[512,512]{1,0:T(8,128)(2,1)} %get-tuple-element.7), channel_id=1, source_target_pairs={{4,2},{8,6},{12,10},{16,14},{20,18},{24,22},{28,26},{3,4},{7,8},{1... | collective-permute-start | bytes 1572872 | tf_op jit(solution)/shard_map/ppermute | solution.py:96
  101.9 1.3 collective-permute-start.7
  103.2 29.4 %all-to-all-done = bf16[4,512,512]{2,1,0:T(8,128)(2,1)S(1)} async-done(((bf16[4,512,512]{2,1,0:T(8,128)(2,1)}), bf16[4,512,512]{2,1,0:T(8,128)(2,1)S(1)}, u32[]{:S(2)}, u32[]{:S(2)}) %all-to-all-start) | async-done | bytes 2097184 | tf_op jit(solution)/shard_map/all_to_all | solution.py:83
  132.9 1.7 %multiply_reduce_fusion = f32[512]{0:T(512)S(1)} fusion(bf16[512,512]{1,0:T(8,128)(2,1)} %collective-permute-done.7, bf16[512,512]{1,0:T(8,128)(2,1)} %collective-permute-done.6, bf16[512,512]{1,0:T(8,128)(2,1)S(1)} %collective-permute-done.5, f32[512,512]{1,0:T(8,128)S(1)} %convert_reduce_fusion, bf16[512,512]{1,0:T(8,128)(2,1)S(1)} %collective-permute-done.4), kind=kLoop, calls=%fused_computation.165 | loop fusion | flops 2620928 | bytes 3147776 | tf_op jit(solution)/shard_map/reduce_sum | solution.py:97
  134.6 2.5 %broadcast_divide_fusion = f32[512,512]{1,0:T(8,128)} fusion(f32[512]{0:T(512)S(1)} %add_sqrt_fusion.1, bf16[512,512]{1,0:T(8,128)(2,1)} %collective-permute-done.7, bf16[512,512]{1,0:T(8,128)(2,1)} %collective-permute-done.6, bf16[512,512]{1,0:T(8,128)(2,1)S(1)} %collective-permute-done.5, f32[512,512]{1,0:T(8,128)S(1)} %convert_reduce_fusion, ...), kind=kLoop, calls=%fused_computation.253 | loop fusion | flops 2359296 | bytes 4196352 | tf_op jit(solution)/shard_map/div | solution.py:98
  (80 shorter events, 16.8 us)
Async XLA Ops:
  0.0 3.4 %copy-start.3 = (bf16[4096,512]{1,0:T(8,128)(2,1)S(1)}, bf16[4096,512]{1,0:T(8,128)(2,1)}, u32[]{:S(2)}) copy-start(bf16[4096,512]{1,0:T(8,128)(2,1)} %param.5) | copy-start | bytes 12582916
  3.5 15.2 %copy-start.4 = (s32[4096]{0:T(1024)S(1)}, s32[4096]{0:T(1024)}, u32[]{:S(2)}) copy-start(s32[4096]{0:T(1024)} %param.6) | copy-start | bytes 49156
  3.5 15.2 %copy-start.5 = (s32[4096]{0:T(1024)S(1)}, s32[4096]{0:T(1024)}, u32[]{:S(2)}) copy-start(s32[4096]{0:T(1024)} %param.7) | copy-start | bytes 49156
  3.5 15.2 %copy-start.6 = (s32[4096]{0:T(1024)S(1)}, s32[4096]{0:T(1024)}, u32[]{:S(2)}) copy-start(s32[4096]{0:T(1024)} %param.9) | copy-start | bytes 49156
  4.5 1.9 %copy-start = (bf16[4096,512]{1,0:T(8,128)(2,1)}, bf16[4096,512]{1,0:T(8,128)(2,1)S(1)}, u32[]{:S(2)}) copy-start(bf16[4096,512]{1,0:T(8,128)(2,1)S(1)} %fusion.1) | copy-start | bytes 12582916
  6.4 25.4 %collective-permute-start.1 = (bf16[256,512]{1,0:T(8,128)(2,1)S(1)}, bf16[256,512]{1,0:T(8,128)(2,1)S(1)}, u32[]{:S(2)}, u32[]{:S(2)}) collective-permute-start(bf16[256,512]{1,0:T(8,128)(2,1)S(1)} %get-tuple-element.12), channel_id=1, source_target_pairs={{0,1},{1,2},{2,3},{3,4},{4,5},{5,6},{6,7},{7,8},{8,9},{9,10},{10,1... | collective-permute-start | bytes 786440 | tf_op jit(solution)/shard_map/ppermute | solution.py:19
  10.2 21.7 %collective-permute-start.3 = (bf16[256,512]{1,0:T(8,128)(2,1)S(1)}, bf16[256,512]{1,0:T(8,128)(2,1)S(1)}, u32[]{:S(2)}, u32[]{:S(2)}) collective-permute-start(bf16[256,512]{1,0:T(8,128)(2,1)S(1)} %get-tuple-element.11), channel_id=1, source_target_pairs={{1,0},{2,1},{3,2},{4,3},{5,4},{6,5},{7,6},{8,7},{9,8},{10,9},{11,1... | collective-permute-start | bytes 786440 | tf_op jit(solution)/shard_map/ppermute | solution.py:22
  12.8 6.0 %collective-permute-start = (bf16[256]{0:T(256)(128)(2,1)S(1)}, bf16[256]{0:T(256)(128)(2,1)S(1)}, u32[]{:S(2)}, u32[]{:S(2)}) collective-permute-start(bf16[256]{0:T(256)(128)(2,1)S(1)} %get-tuple-element.62), channel_id=1, source_target_pairs={{0,1},{1,2},{2,3},{3,4},{4,5},{5,6},{6,7},{7,8},{8,9},{9,10},{10,1... | collective-permute-start | bytes 1544 | tf_op jit(solution)/shard_map/ppermute | solution.py:19
  16.4 4.9 %collective-permute-start.2 = (bf16[256]{0:T(256)(128)(2,1)S(1)}, bf16[256]{0:T(256)(128)(2,1)S(1)}, u32[]{:S(2)}, u32[]{:S(2)}) collective-permute-start(bf16[256]{0:T(256)(128)(2,1)S(1)} %get-tuple-element.61), channel_id=1, source_target_pairs={{1,0},{2,1},{3,2},{4,3},{5,4},{6,5},{7,6},{8,7},{9,8},{10,9},{11,1... | collective-permute-start | bytes 1544 | tf_op jit(solution)/shard_map/ppermute | solution.py:22
  18.7 4.5 %copy-start.1 = (bf16[4096,512]{1,0:T(8,128)(2,1)S(1)}, bf16[4096,512]{1,0:T(8,128)(2,1)}, u32[]{:S(2)}) copy-start(bf16[4096,512]{1,0:T(8,128)(2,1)} %copy-done) | copy-start | bytes 12582916
  85.6 1.9 %copy-start.2 = (bf16[4096,512]{1,0:T(8,128)(2,1)}, bf16[4096,512]{1,0:T(8,128)(2,1)S(1)}, u32[]{:S(2)}) copy-start(bf16[4096,512]{1,0:T(8,128)(2,1)S(1)} %convert_element_type.170) | copy-start | bytes 12582916
  89.0 43.5 %all-to-all-start = ((bf16[4,512,512]{2,1,0:T(8,128)(2,1)}), bf16[4,512,512]{2,1,0:T(8,128)(2,1)S(1)}, u32[]{:S(2)}, u32[]{:S(2)}) async-start(bf16[4,512,512]{2,1,0:T(8,128)(2,1)} %bitcast.33), calls=%async_computation | async-start | bytes 4194304 | tf_op jit(solution)/shard_map/all_to_all | solution.py:83
  98.4 34.5 %collective-permute-start.4 = (bf16[512,512]{1,0:T(8,128)(2,1)}, bf16[512,512]{1,0:T(8,128)(2,1)S(1)}, u32[]{:S(2)}, u32[]{:S(2)}) collective-permute-start(bf16[512,512]{1,0:T(8,128)(2,1)} %get-tuple-element.5), channel_id=1, source_target_pairs={{4,0},{8,4},{12,8},{16,12},{20,16},{24,20},{28,24},{3,6},{7,10},{1... | collective-permute-start | bytes 1572872 | tf_op jit(solution)/shard_map/ppermute | solution.py:96
  99.1 33.8 %collective-permute-start.5 = (bf16[512,512]{1,0:T(8,128)(2,1)}, bf16[512,512]{1,0:T(8,128)(2,1)S(1)}, u32[]{:S(2)}, u32[]{:S(2)}) collective-permute-start(bf16[512,512]{1,0:T(8,128)(2,1)} %get-tuple-element.6), channel_id=1, source_target_pairs={{4,1},{8,5},{12,9},{16,13},{20,17},{24,21},{28,25},{3,7},{7,11},{1... | collective-permute-start | bytes 1572872 | tf_op jit(solution)/shard_map/ppermute | solution.py:96
  100.4 32.5 %collective-permute-start.6 = (bf16[512,512]{1,0:T(8,128)(2,1)}, bf16[512,512]{1,0:T(8,128)(2,1)}, u32[]{:S(2)}, u32[]{:S(2)}) collective-permute-start(bf16[512,512]{1,0:T(8,128)(2,1)} %get-tuple-element.7), channel_id=1, source_target_pairs={{4,2},{8,6},{12,10},{16,14},{20,18},{24,22},{28,26},{3,4},{7,8},{1... | collective-permute-start | bytes 1572872 | tf_op jit(solution)/shard_map/ppermute | solution.py:96
  101.9 31.0 %collective-permute-start.7 = (bf16[512,512]{1,0:T(8,128)(2,1)}, bf16[512,512]{1,0:T(8,128)(2,1)}, u32[]{:S(2)}, u32[]{:S(2)}) collective-permute-start(bf16[512,512]{1,0:T(8,128)(2,1)} %get-tuple-element.8), channel_id=1, source_target_pairs={{4,3},{8,7},{12,11},{16,15},{20,19},{24,23},{28,27},{3,5},{7,9},{1... | collective-permute-start | bytes 1572872 | tf_op jit(solution)/shard_map/ppermute | solution.py:96

commit v2 on v0

v2 whole, which is shorter than its diff:
```python
import functools

import jax
import jax.numpy as jnp
from jax import lax
from jax.experimental import pallas as pl
from jax.experimental.pallas import tpu as pltpu
from jax.sharding import PartitionSpec as P

BLOCK = 256
CL_DEV = 512
TILE = 256
MESH = pl.DeviceIdType.MESH

sharpness = 3.0


def remote(src, dst, send_sem, recv_sem, device):
    return pltpu.make_async_remote_copy(
        src_ref=src,
        dst_ref=dst,
        send_sem=send_sem,
        recv_sem=recv_sem,
        device_id=device,
        device_id_type=MESH,
    )


def kernel(
    M,
    R,
    x_hbm,
    reach_ref,
    live_ref,
    ids_ref,
    out_ref,
    raw,
    ext,
    cons,
    halo,
    live_in,
    slots,
    own,
    edge_out,
    edge_in,
    pair_out,
    pair_in,
    cross_out,
    cross_in,
    load_sem,
    halo_send,
    halo_recv,
    edge_send,
    edge_recv,
    pair_send,
    pair_recv,
    cross_send,
    cross_recv,
):
    rows, dim = raw.shape
    blocks = rows // BLOCK
    H = R // 2
    per_range = CL_DEV * R
    f32 = jnp.float32
    m, r = lax.axis_index("mz"), lax.axis_index("rep")
    flat = m * R + r
    h, c = r // 2, r % 2
    has_prev, has_next = flat > 0, flat < M * R - 1
    prev = ((flat - 1) // R, (flat + R - 1) % R)
    after = ((flat + 1) // R, (flat + 1) % R)
    partner = (m, 2 * h + 1 - c)
    first, last = r == 0, r == R - 1
    lower, upper = m > 0, m < M - 1
    sends_edge = jnp.logical_or(jnp.logical_and(first, lower), jnp.logical_and(last, upper))
    edge_mz = jnp.where(first, m - 1, m + 1)
    edge_slot = jnp.where(first, 0, 1)

    def load(i):
        at = pl.ds(pl.multiple_of(i * BLOCK, BLOCK), BLOCK)
        return pltpu.make_async_copy(x_hbm.at[at], raw.at[at], load_sem.at[i])

    barrier = pltpu.get_barrier_semaphore()

    def greet(device):
        pl.semaphore_signal(barrier, inc=1, device_id=device, device_id_type=MESH)

    greet(partner)
    for j in range(1, H):
        greet((m, 2 * ((h + j) % H) + c))

    @pl.when(has_prev)
    def _():
        greet(prev)

    @pl.when(has_next)
    def _():
        greet(after)

    @pl.when(sends_edge)
    def _():
        for k in range(R):
            greet((edge_mz, k))

    @pl.when(upper)
    def _():
        greet((m + 1, 0))

    @pl.when(lower)
    def _():
        greet((m - 1, R - 1))

    for i in range(blocks):
        load(i).start()

    as_int = lambda flag: jnp.where(flag, 1, 0)
    pl.semaphore_wait(
        barrier,
        H
        + as_int(has_prev)
        + as_int(has_next)
        + as_int(upper)
        + as_int(lower)
        + R * as_int(sends_edge),
    )

    tail = pl.ds(rows - BLOCK, BLOCK)
    head = pl.ds(0, BLOCK)
    to_next = [
        remote(x_hbm.at[tail], halo.at[0], halo_send.at[0], halo_recv.at[0], after),
        remote(live_ref, live_in.at[0], halo_send.at[1], halo_recv.at[1], after),
    ]
    to_prev = [
        remote(x_hbm.at[head], halo.at[1], halo_send.at[2], halo_recv.at[2], prev),
        remote(live_ref, live_in.at[1], halo_send.at[3], halo_recv.at[3], prev),
    ]

    @pl.when(has_next)
    def _():
        for copy in to_next:
            copy.start()

    @pl.when(has_prev)
    def _():
        for copy in to_prev:
            copy.start()

    def unit(block):
        values = block.astype(f32)
        norm = jnp.sqrt(jnp.sum(values * values, axis=1, keepdims=True) + 1e-06)
        return (values * (1.0 / norm)).astype(jnp.bfloat16)

    live = live_ref[0:1, 0:1]
    position = lax.broadcasted_iota(jnp.int32, (1, rows), 1)
    local = ids_ref[...] - m * per_range
    slot = jnp.where(local < 0, local + 2 * per_range, local)
    slots[...] = jnp.where(position < live, slot, -1)

    def normalise(i, carry):
        load(i).wait()
        at = pl.multiple_of(i * BLOCK, BLOCK)
        ext[pl.ds(at + BLOCK, BLOCK), :] = unit(raw[pl.ds(at, BLOCK), :])
        return carry

    lax.fori_loop(0, blocks, normalise, 0)

    def band(i, low_live, high_live):
        at = pl.multiple_of(i * BLOCK, BLOCK)
        keys = ext[pl.ds(at, 3 * BLOCK), :]
        queries = ext[pl.ds(at + BLOCK, BLOCK), :]
        scores = lax.dot_general(
            queries, keys, (((1,), (1,)), ((), ())), preferred_element_type=f32
        )
        reach = reach_ref[...]
        lane = lax.broadcasted_iota(jnp.int32, reach.shape, 1)
        back = jnp.sum(jnp.where(lane == i, reach, 0.0), axis=1, keepdims=True)
        ahead = jnp.sum(jnp.where(lane == i + blocks, reach, 0.0), axis=1, keepdims=True)
        query = lax.broadcasted_iota(jnp.int32, (BLOCK, 1), 0).astype(f32) + BLOCK
        key_lane = lax.broadcasted_iota(jnp.int32, (1, 3 * BLOCK), 1)
        key_pos = key_lane + (at - BLOCK)
        limit = jnp.where(
            key_pos < 0, low_live - rows, jnp.where(key_pos >= rows, high_live + rows, live)
        )
        key = jnp.where(key_pos < limit, key_lane.astype(f32), f32(-1e6))
        inside = (key >= query - back) & (key <= query + ahead)
        keep = inside | (key_lane.astype(f32) == query)
        weight = jnp.where(keep, jnp.exp(sharpness * (scores - 1.0)), f32(0.0))
        total = jnp.sum(weight, axis=1, keepdims=True)
        mixed = jnp.dot(weight.astype(jnp.bfloat16), keys, preferred_element_type=f32)
        cons[pl.ds(at, BLOCK), :] = (mixed * (1.0 / total)).astype(jnp.bfloat16)

    def inner(i, carry):
        band(i, live, live)
        return carry

    lax.fori_loop(1, blocks - 1, inner, 0)

    @pl.when(has_prev)
    def _():
        for copy in to_next:
            copy.wait_recv()
        ext[0:BLOCK, :] = unit(halo[0])

    @pl.when(jnp.logical_not(has_prev))
    def _():
        ext[0:BLOCK, :] = jnp.zeros((BLOCK, dim), jnp.bfloat16)
        live_in[0] = jnp.zeros(live_in.shape[1:], jnp.int32)

    @pl.when(has_next)
    def _():
        for copy in to_prev:
            copy.wait_recv()
        ext[rows + BLOCK : rows + 2 * BLOCK, :] = unit(halo[1])

    @pl.when(jnp.logical_not(has_next))
    def _():
        ext[rows + BLOCK : rows + 2 * BLOCK, :] = jnp.zeros((BLOCK, dim), jnp.bfloat16)
        live_in[1] = jnp.zeros(live_in.shape[1:], jnp.int32)

    low_live, high_live = live_in[0][0:1, 0:1], live_in[1][0:1, 0:1]

    def outer(j, carry):
        band(j * (blocks - 1), low_live, high_live)
        return carry

    lax.fori_loop(0, 2, outer, 0)

    def partial(base):
        row = lax.broadcasted_iota(jnp.int32, (TILE, rows), 0)
        pick = jnp.where(slots[...] - base == row, f32(1.0), f32(0.0)).astype(jnp.bfloat16)
        return jnp.dot(pick, cons[...], preferred_element_type=f32)

    def each_tile(piece, store):
        def body(t, carry):
            at = pl.multiple_of(t * TILE, TILE)
            store(pl.ds(at, TILE), partial(piece * CL_DEV + at))
            return carry

        lax.fori_loop(0, CL_DEV // TILE, body, 0)

    def edge_copy(j):
        k = (j + jnp.where(first, R // 2, 0)) % R
        return k, remote(
            edge_out.at[j],
            edge_in.at[edge_slot],
            edge_send.at[j],
            edge_recv.at[edge_slot],
            (edge_mz, k),
        )

    @pl.when(sends_edge)
    def _():
        def body(j, carry):
            k, copy = edge_copy(j)

            def store(at, value):
                edge_out[j, at, :] = value.astype(jnp.bfloat16)

            each_tile(R + k, store)
            copy.start()
            return carry

        lax.fori_loop(0, R, body, 0)

    def pair_copy(j):
        return remote(
            pair_out.at[j], pair_in.at[j], pair_send.at[j], pair_recv.at[j], partner
        )

    def cross_copy(j):
        return remote(
            cross_out.at[j - 1],
            cross_in.at[j - 1],
            cross_send.at[j - 1],
            cross_recv.at[j - 1],
            (m, 2 * ((h + j) % H) + c),
        )

    def give(j, carry):
        def store(at, value):
            pair_out[j, at, :] = value.astype(jnp.bfloat16)

        each_tile(2 * ((h + j + 1) % H) + 1 - c, store)
        pair_copy(j).start()
        return carry

    lax.fori_loop(0, H, give, 0)

    def keep_own(j, carry):
        def store(at, value):
            own[at, :] = value

        each_tile(2 * ((h + j + 1) % H) + c, store)
        pair_copy(j).wait_recv()

        @pl.when(j < H - 1)
        def _():
            cross_out[j] = (own[...] + pair_in[j].astype(f32)).astype(jnp.bfloat16)
            cross_copy(j + 1).start()

        return carry

    lax.fori_loop(0, H, keep_own, 0)

    own[...] += pair_in[H - 1].astype(f32)
    for j in range(1, H):
        cross_copy(j).wait_recv()
        own[...] += cross_in[j - 1].astype(f32)

    def edge_arrival(side):
        return remote(
            edge_out.at[0], edge_in.at[side], edge_send.at[0], edge_recv.at[side], partner
        )

    @pl.when(upper)
    def _():
        edge_arrival(0).wait_recv()
        own[...] += edge_in[0].astype(f32)

    @pl.when(lower)
    def _():
        edge_arrival(1).wait_recv()
        own[...] += edge_in[1].astype(f32)

    owned = own[...]
    scale = jnp.sqrt(jnp.mean(owned * owned, axis=1, keepdims=True) + 1e-06)
    out_ref[...] = owned * (1.0 / scale)

    @pl.when(has_next)
    def _():
        for copy in to_next:
            copy.wait_send()

    @pl.when(has_prev)
    def _():
        for copy in to_prev:
            copy.wait_send()

    @pl.when(sends_edge)
    def _():
        for j in range(R):
            edge_copy(j)[1].wait_send()

    for j in range(H):
        pair_copy(j).wait_send()
    for j in range(1, H):
        cross_copy(j).wait_send()


def shards(spectra, reach_back, reach_ahead, live, cluster_ids):
    rows, dim = spectra.shape
    M, R = lax.axis_size("mz"), lax.axis_size("rep")
    H = R // 2
    blocks = rows // BLOCK
    reach = jnp.concatenate(
        [reach_back.reshape(blocks, BLOCK), reach_ahead.reshape(blocks, BLOCK)], axis=0
    )
    reach = reach.astype(jnp.float32).T
    piece = (CL_DEV, dim)
    half = jnp.bfloat16
    dma = pltpu.SemaphoreType.DMA
    vmem = pl.BlockSpec(memory_space=pltpu.VMEM)
    return pl.pallas_call(
        functools.partial(kernel, M, R),
        out_shape=jax.ShapeDtypeStruct((CL_DEV, dim), jnp.float32),
        in_specs=[pl.BlockSpec(memory_space=pl.ANY), vmem, vmem, vmem],
        out_specs=vmem,
        scratch_shapes=[
            pltpu.VMEM((rows, dim), half),
            pltpu.VMEM((rows + 2 * BLOCK, dim), half),
            pltpu.VMEM((rows, dim), half),
            pltpu.VMEM((2, BLOCK, dim), half),
            pltpu.VMEM((2, 8, 128), jnp.int32),
            pltpu.VMEM((1, rows), jnp.int32),
            pltpu.VMEM(piece, jnp.float32),
            pltpu.VMEM((R,) + piece, half),
            pltpu.VMEM((2,) + piece, half),
            pltpu.VMEM((H,) + piece, half),
            pltpu.VMEM((H,) + piece, half),
            pltpu.VMEM((max(H - 1, 1),) + piece, half),
            pltpu.VMEM((max(H - 1, 1),) + piece, half),
            dma((blocks,)),
            dma((4,)),
            dma((4,)),
            dma((R,)),
            dma((2,)),
            dma((H,)),
            dma((H,)),
            dma((max(H - 1, 1),)),
            dma((max(H - 1, 1),)),
        ],
        compiler_params=pltpu.CompilerParams(
            collective_id=0, has_side_effects=True, vmem_limit_bytes=56 * 1024 * 1024
        ),
        name="consensus",
    )(
        spectra,
        reach,
        jnp.broadcast_to(live.reshape(1, 1), (8, 128)),
        cluster_ids.reshape(1, rows),
    )


def solution(mesh):
    return jax.shard_map(
        shards,
        mesh=mesh,
        in_specs=(
            P(("mz", "rep"), None),
            P(("mz", "rep")),
            P(("mz", "rep")),
            P(("mz", "rep")),
            P(("mz", "rep")),
        ),
        out_specs=P(("mz", "rep"), None),
        check_vma=False,
    )
```

time: 221 us -> 58.1 us (0.26)
  blocking collectives: 98.3 us -> 0 us
  Pallas kernels: 0 us -> 51.7 us
  other arithmetic: 51.2 us -> 0.01 us
  matrix products: 29.5 us -> 0 us
  waiting for transfers between devices: 19.7 us -> 0 us
  starting transfers between devices: 16.6 us -> 0 us
  local copies, waits for them, and re-layouts: 2.48 us -> 5.05 us
    all_to_all x1 -> x0, blocking collectives: 98.3 us -> none  [shards(): lax.all_to_all(stacked, 'rep', split_axis=1, concat_axis=1, tiled=True)]
    pallas_call x0 -> x1, Pallas kernels: none -> 51.7 us  [shards(): pl.pallas_call(functools.partial(kernel, M, R), out_shape=jax.ShapeDtypeS...]
    scatter-add x1 -> x0, other arithmetic: 32.5 us -> none  [shards(): jax.ops.segment_sum(kept, local_slot, num_segments=3 * per_range)]
    dot_general x32 -> x0, matrix products: 29.5 us -> none  [the longest x16 17.4 us: rows_block(): jnp.dot(weight.astype(jnp.bfloat16), keys, preferred_element_type=jnp.flo...]
    ppermute x6 -> x0, waiting for transfers between devices: 19.7 us -> none  [the longest x2 19.7 us: shifted(): return lax.ppermute(block, axis, route)]
    ppermute x6 -> x0, starting transfers between devices: 16.6 us -> none  [the longest x2 6.69 us: extended(): lax.ppermute(lax.slice_in_dim(block, block.shape[dim] - width, None, axis...]
    slice x1 -> x0, other arithmetic: 8.16 us -> none  [shards(): partial_value[1]]
    another operation x2 -> x0, other arithmetic: 4.17 us -> none  [the longest x1 3.63 us: shards(): jnp.stack([partial_value[1], edge_part]).reshape(2, rep_count, CL_DEV, DIM)]
  transfers between devices with their start and end apart: 6 -> 0, of which waited for: 1 -> 0; matrix products, arithmetic and copies ran while one was open for 7% -> 0% of each run, Pallas kernels for 0% -> 0%
where the time goes in v2:
time: 58.1 us; the launch traced here: 57.4 us
  Pallas kernels  51.7 us (89%)
  local copies, waits for them, and re-layouts  5.05 us (9%)
  between operations  0.66 us (1%)
    pallas_call x1, Pallas kernels, shards(): pl.pallas_call(functools.partial(kernel, M, R), out_shape=jax.ShapeDtypeS...  51.7 us
    unnamed x1, local copies, waits for them, and re-layouts  2.26 us

profile of v2, /device:TPU:3, one launch (start us, length us, event | category | flops | bytes accessed | tf_op | source)
XLA Modules:
  0.0 57.4 jit_solution(5680797674498688644)
XLA Ops:
  0.7 0.6 %broadcast_in_dim.8.live_ref = s32[8,128]{1,0:T(8,128)} broadcast(s32[]{:T(128)} %bitcast.3), dimensions={} | broadcast | bytes 4100 | tf_op jit(solution)/shard_map/broadcast_in_dim | solution.py:398
  1.2 0.7 %reshape.11 = s32[16,256]{1,0:T(8,128)S(1)} reshape(s32[4096]{0:T(1024)} %param.6) | data formatting | bytes 32768 | tf_op jit(solution)/shard_map/reshape | solution.py:355
  2.0 0.7 %reshape.12 = s32[16,256]{1,0:T(8,128)S(1)} reshape(s32[4096]{0:T(1024)} %param.7) | data formatting | bytes 32768 | tf_op jit(solution)/shard_map/reshape | solution.py:355
  2.7 0.8 %copy.9 = f32[32,256]{0,1:T(8,128)} copy(f32[32,256]{1,0:T(8,128)S(1)} %add_convert_fusion) | data formatting | bytes 65536 | tf_op jit(solution)/shard_map/convert_element_type | solution.py:357
  3.5 51.7 %consensus.1 = f32[512,512]{1,0:T(8,128)} custom-call(bf16[4096,512]{1,0:T(8,128)(2,1)} %x_hbm.1, f32[256,32]{1,0:T(8,128)} %bitcast.4, s32[8,128]{1,0:T(8,128)} %broadcast_in_dim.8.live_ref, s32[1,4096]{1,0:T(1,128)} %bitcast.5), custom_call_target="tpu_custom_call" | custom-call | tf_op jit(solution)/shard_map/consensus/pallas_call | solution.py:362
  55.2 2.3 %copy.12 = f32[512,512]{1,0:T(8,128)} copy(f32[512,512]{1,0:T(8,128)} %consensus.1) | data formatting | bytes 2097152
  (1 shorter events, 0.0 us)

commit v3 on v2

--- a/solution.py
+++ b/solution.py
@@ -10,6 +10,7 @@
 BLOCK = 256
 CL_DEV = 512
 TILE = 256
+LANES = 128
 MESH = pl.DeviceIdType.MESH
 
 sharpness = 3.0
@@ -30,7 +31,8 @@
     M,
     R,
     x_hbm,
-    reach_ref,
+    back_ref,
+    ahead_ref,
     live_ref,
     ids_ref,
     out_ref,
@@ -38,7 +40,9 @@
     ext,
     cons,
     halo,
+    live_out,
     live_in,
+    reach_t,
     slots,
     own,
     edge_out,
@@ -112,6 +116,8 @@
     for i in range(blocks):
         load(i).start()
 
+    live = live_ref[0]
+    live_out[...] = jnp.full(live_out.shape, live, jnp.int32)
     as_int = lambda flag: jnp.where(flag, 1, 0)
     pl.semaphore_wait(
         barrier,
@@ -127,11 +133,11 @@
     head = pl.ds(0, BLOCK)
     to_next = [
         remote(x_hbm.at[tail], halo.at[0], halo_send.at[0], halo_recv.at[0], after),
-        remote(live_ref, live_in.at[0], halo_send.at[1], halo_recv.at[1], after),
+        remote(live_out, live_in.at[0], halo_send.at[1], halo_recv.at[1], after),
     ]
     to_prev = [
         remote(x_hbm.at[head], halo.at[1], halo_send.at[2], halo_recv.at[2], prev),
-        remote(live_ref, live_in.at[1], halo_send.at[3], halo_recv.at[3], prev),
+        remote(live_out, live_in.at[1], halo_send.at[3], halo_recv.at[3], prev),
     ]
 
     @pl.when(has_next)
@@ -149,19 +155,31 @@
         norm = jnp.sqrt(jnp.sum(values * values, axis=1, keepdims=True) + 1e-06)
         return (values * (1.0 / norm)).astype(jnp.bfloat16)
 
-    live = live_ref[0:1, 0:1]
-    position = lax.broadcasted_iota(jnp.int32, (1, rows), 1)
+    lines, lanes = ids_ref.shape
+    reach = jnp.concatenate(
+        [
+            back_ref[...].astype(f32),
+            ahead_ref[...].astype(f32),
+            jnp.zeros((lanes - 2 * lines, lanes), f32),
+        ],
+        axis=0,
+    )
+    reach_t[...] = reach.T
+    position = lax.broadcasted_iota(jnp.int32, (lines, lanes), 0) * lanes
+    position = position + lax.broadcasted_iota(jnp.int32, (lines, lanes), 1)
     local = ids_ref[...] - m * per_range
     slot = jnp.where(local < 0, local + 2 * per_range, local)
-    slots[...] = jnp.where(position < live, slot, -1)
-
-    def normalise(i, carry):
-        load(i).wait()
+    slot = jnp.where(position < live, slot, -1)
+    for k in range(lines):
+        slots[:, k * lanes : (k + 1) * lanes] = slot[k : k + 1, :]
+
+    def normalise(i):
         at = pl.multiple_of(i * BLOCK, BLOCK)
         ext[pl.ds(at + BLOCK, BLOCK), :] = unit(raw[pl.ds(at, BLOCK), :])
-        return carry
-
-    lax.fori_loop(0, blocks, normalise, 0)
+
+    for i in range(4):
+        load(i).wait()
+        normalise(i)
 
     def band(i, low_live, high_live):
         at = pl.multiple_of(i * BLOCK, BLOCK)
@@ -170,10 +188,19 @@
         scores = lax.dot_general(
             queries, keys, (((1,), (1,)), ((), ())), preferred_element_type=f32
         )
-        reach = reach_ref[...]
-        lane = lax.broadcasted_iota(jnp.int32, reach.shape, 1)
-        back = jnp.sum(jnp.where(lane == i, reach, 0.0), axis=1, keepdims=True)
-        ahead = jnp.sum(jnp.where(lane == i + blocks, reach, 0.0), axis=1, keepdims=True)
+        table = reach_t[...]
+        lane = lax.broadcasted_iota(jnp.int32, table.shape, 1)
+        per_block = BLOCK // lanes
+
+        def column(first_line):
+            pick = [
+                jnp.sum(jnp.where(lane == first_line + k, table, 0.0), axis=1, keepdims=True)
+                for k in range(per_block)
+            ]
+            return jnp.concatenate(pick, axis=0)
+
+        back = column(i * per_block)
+        ahead = column(lines + i * per_block)
         query = lax.broadcasted_iota(jnp.int32, (BLOCK, 1), 0).astype(f32) + BLOCK
         key_lane = lax.broadcasted_iota(jnp.int32, (1, 3 * BLOCK), 1)
         key_pos = key_lane + (at - BLOCK)
@@ -188,11 +215,18 @@
         mixed = jnp.dot(weight.astype(jnp.bfloat16), keys, preferred_element_type=f32)
         cons[pl.ds(at, BLOCK), :] = (mixed * (1.0 / total)).astype(jnp.bfloat16)
 
-    def inner(i, carry):
+    def inner(p, carry):
+        for k in range(2):
+            load(4 + 2 * p + k).wait()
+        for k in range(2):
+            band(1 + 2 * p + k, live, live)
+        for k in range(2):
+            normalise(4 + 2 * p + k)
+        return carry
+
+    lax.fori_loop(0, (blocks - 4) // 2, inner, 0)
+    for i in range(blocks - 3, blocks - 1):
         band(i, live, live)
-        return carry
-
-    lax.fori_loop(1, blocks - 1, inner, 0)
 
     @pl.when(has_prev)
     def _():
@@ -218,108 +252,121 @@
 
     low_live, high_live = live_in[0][0:1, 0:1], live_in[1][0:1, 0:1]
 
-    def outer(j, carry):
-        band(j * (blocks - 1), low_live, high_live)
-        return carry
-
-    lax.fori_loop(0, 2, outer, 0)
+    band(0, low_live, live)
+    band(blocks - 1, live, high_live)
 
     def partial(base):
         row = lax.broadcasted_iota(jnp.int32, (TILE, rows), 0)
         pick = jnp.where(slots[...] - base == row, f32(1.0), f32(0.0)).astype(jnp.bfloat16)
         return jnp.dot(pick, cons[...], preferred_element_type=f32)
 
-    def each_tile(piece, store):
+    tiles = CL_DEV // TILE
+
+    def each_tile(piece, use):
         def body(t, carry):
             at = pl.multiple_of(t * TILE, TILE)
-            store(pl.ds(at, TILE), partial(piece * CL_DEV + at))
+            use(t, pl.ds(at, TILE), partial(piece * CL_DEV + at))
             return carry
 
-        lax.fori_loop(0, CL_DEV // TILE, body, 0)
-
-    def edge_copy(j):
+        lax.fori_loop(0, tiles, body, 0)
+
+    def edge_copy(j, t):
         k = (j + jnp.where(first, R // 2, 0)) % R
-        return k, remote(
-            edge_out.at[j],
-            edge_in.at[edge_slot],
-            edge_send.at[j],
-            edge_recv.at[edge_slot],
+        at = pl.ds(pl.multiple_of(t * TILE, TILE), TILE)
+        return remote(
+            edge_out.at[j, at],
+            edge_in.at[edge_slot, at],
+            edge_send.at[j, t],
+            edge_recv.at[edge_slot, t],
             (edge_mz, k),
         )
 
-    @pl.when(sends_edge)
-    def _():
-        def body(j, carry):
-            k, copy = edge_copy(j)
-
-            def store(at, value):
-                edge_out[j, at, :] = value.astype(jnp.bfloat16)
-
-            each_tile(R + k, store)
-            copy.start()
-            return carry
-
-        lax.fori_loop(0, R, body, 0)
-
-    def pair_copy(j):
+    def edges(start, stop):
+        @pl.when(sends_edge)
+        def _():
+            def body(j, carry):
+                def use(t, at, value):
+                    edge_out[j, at, :] = value.astype(jnp.bfloat16)
+                    edge_copy(j, t).start()
+
+                each_tile(R + (j + jnp.where(first, R // 2, 0)) % R, use)
+                return carry
+
+            lax.fori_loop(start, stop, body, 0)
+
+    def pair_copy(j, t):
+        at = pl.ds(pl.multiple_of(t * TILE, TILE), TILE)
         return remote(
-            pair_out.at[j], pair_in.at[j], pair_send.at[j], pair_recv.at[j], partner
+            pair_out.at[j, at],
+            pair_in.at[j, at],
+            pair_send.at[j, t],
+            pair_recv.at[j, t],
+            partner,
         )
 
-    def cross_copy(j):
+    def cross_copy(j, t):
+        at = pl.ds(pl.multiple_of(t * TILE, TILE), TILE)
         return remote(
-            cross_out.at[j - 1],
-            cross_in.at[j - 1],
-            cross_send.at[j - 1],
-            cross_recv.at[j - 1],
-            (m, 2 * ((h + j) % H) + c),
+            cross_out.at[j, at],
+            cross_in.at[j, at],
+            cross_send.at[j, t],
+            cross_recv.at[j, t],
+            (m, 2 * ((h + j + 1) % H) + c),
         )
 
-    def give(j, carry):
-        def store(at, value):
+    def give(j):
+        def use(t, at, value):
             pair_out[j, at, :] = value.astype(jnp.bfloat16)
-
-        each_tile(2 * ((h + j + 1) % H) + 1 - c, store)
-        pair_copy(j).start()
-        return carry
-
-    lax.fori_loop(0, H, give, 0)
-
-    def keep_own(j, carry):
-        def store(at, value):
-            own[at, :] = value
-
-        each_tile(2 * ((h + j + 1) % H) + c, store)
-        pair_copy(j).wait_recv()
-
-        @pl.when(j < H - 1)
-        def _():
-            cross_out[j] = (own[...] + pair_in[j].astype(f32)).astype(jnp.bfloat16)
-            cross_copy(j + 1).start()
-
-        return carry
-
-    lax.fori_loop(0, H, keep_own, 0)
-
+            pair_copy(j, t).start()
+
+        each_tile(2 * ((h + j + 1) % H) + 1 - c, use)
+
+    edges(0, R // 2)
+    for j in range(H - 1):
+        give(j)
+
+        def forward(t, at, value):
+            pair_copy(j, t).wait_recv()
+            value = value + pair_in[j, at, :].astype(f32)
+            cross_out[j, at, :] = value.astype(jnp.bfloat16)
+            cross_copy(j, t).start()
+
+        each_tile(2 * ((h + j + 1) % H) + c, forward)
+    edges(R // 2, R)
+    give(H - 1)
+
+    def hold(t, at, value):
+        own[at, :] = value
+
+    each_tile(2 * h + c, hold)
+
+    for t in range(tiles):
+        pair_copy(H - 1, t).wait_recv()
     own[...] += pair_in[H - 1].astype(f32)
-    for j in range(1, H):
-        cross_copy(j).wait_recv()
-        own[...] += cross_in[j - 1].astype(f32)
+    for j in range(H - 1):
+        for t in range(tiles):
+            cross_copy(j, t).wait_recv()
+        own[...] += cross_in[j].astype(f32)
 
     def edge_arrival(side):
-        return remote(
-            edge_out.at[0], edge_in.at[side], edge_send.at[0], edge_recv.at[side], partner
-        )
+        for t in range(tiles):
+            at = pl.ds(t * TILE, TILE)
+            remote(
+                edge_out.at[0, at],
+                edge_in.at[side, at],
+                edge_send.at[0, t],
+                edge_recv.at[side, t],
+                partner,
+            ).wait_recv()
+        own[...] += edge_in[side].astype(f32)
 
     @pl.when(upper)
     def _():
-        edge_arrival(0).wait_recv()
-        own[...] += edge_in[0].astype(f32)
+        edge_arrival(0)
 
     @pl.when(lower)
     def _():
-        edge_arrival(1).wait_recv()
-        own[...] += edge_in[1].astype(f32)
+        edge_arrival(1)
 
     owned = own[...]
     scale = jnp.sqrt(jnp.mean(owned * owned, axis=1, keepdims=True) + 1e-06)
@@ -338,12 +385,14 @@
     @pl.when(sends_edge)
     def _():
         for j in range(R):
-            edge_copy(j)[1].wait_send()
-
-    for j in range(H):
-        pair_copy(j).wait_send()
-    for j in range(1, H):
-        cross_copy(j).wait_send()
+            for t in range(tiles):
+                edge_copy(j, t).wait_send()
+
+    for t in range(tiles):
+        for j in range(H):
+            pair_copy(j, t).wait_send()
+        for j in range(H - 1):
+            cross_copy(j, t).wait_send()
 
 
 def shards(spectra, reach_back, reach_ahead, live, cluster_ids):
@@ -351,10 +400,8 @@
     M, R = lax.axis_size("mz"), lax.axis_size("rep")
     H = R // 2
     blocks = rows // BLOCK
-    reach = jnp.concatenate(
-        [reach_back.reshape(blocks, BLOCK), reach_ahead.reshape(blocks, BLOCK)], axis=0
-    )
-    reach = reach.astype(jnp.float32).T
+    tiles = CL_DEV // TILE
+    lines = rows // LANES
     piece = (CL_DEV, dim)
     half = jnp.bfloat16
     dma = pltpu.SemaphoreType.DMA
@@ -362,14 +409,22 @@
     return pl.pallas_call(
         functools.partial(kernel, M, R),
         out_shape=jax.ShapeDtypeStruct((CL_DEV, dim), jnp.float32),
-        in_specs=[pl.BlockSpec(memory_space=pl.ANY), vmem, vmem, vmem],
+        in_specs=[
+            pl.BlockSpec(memory_space=pl.ANY),
+            vmem,
+            vmem,
+            pl.BlockSpec(memory_space=pltpu.SMEM),
+            vmem,
+        ],
         out_specs=vmem,
         scratch_shapes=[
             pltpu.VMEM((rows, dim), half),
             pltpu.VMEM((rows + 2 * BLOCK, dim), half),
             pltpu.VMEM((rows, dim), half),
             pltpu.VMEM((2, BLOCK, dim), half),
-            pltpu.VMEM((2, 8, 128), jnp.int32),
+            pltpu.VMEM((8, LANES), jnp.int32),
+            pltpu.VMEM((2, 8, LANES), jnp.int32),
+            pltpu.VMEM((LANES, LANES), jnp.float32),
             pltpu.VMEM((1, rows), jnp.int32),
             pltpu.VMEM(piece, jnp.float32),
             pltpu.VMEM((R,) + piece, half),
@@ -381,12 +436,12 @@
             dma((blocks,)),
             dma((4,)),
             dma((4,)),
-            dma((R,)),
-            dma((2,)),
-            dma((H,)),
-            dma((H,)),
-            dma((max(H - 1, 1),)),
-            dma((max(H - 1, 1),)),
+            dma((R, tiles)),
+            dma((2, tiles)),
+            dma((H, tiles)),
+            dma((H, tiles)),
+            dma((max(H - 1, 1), tiles)),
+            dma((max(H - 1, 1), tiles)),
         ],
         compiler_params=pltpu.CompilerParams(
             collective_id=0, has_side_effects=True, vmem_limit_bytes=56 * 1024 * 1024
@@ -394,9 +449,10 @@
         name="consensus",
     )(
         spectra,
-        reach,
-        jnp.broadcast_to(live.reshape(1, 1), (8, 128)),
-        cluster_ids.reshape(1, rows),
+        reach_back.reshape(lines, LANES),
+        reach_ahead.reshape(lines, LANES),
+        live,
+        cluster_ids.reshape(lines, LANES),
     )
 
 

time: 58.1 us -> 49.5 us (0.85)
  Pallas kernels: 51.7 us -> 46.2 us
  local copies, waits for them, and re-layouts: 5.05 us -> 2.26 us
    pallas_call x1, Pallas kernels: 51.7 us -> 46.2 us  [shards(): pl.pallas_call(functools.partial(kernel, M, R), out_shape=jax.ShapeDtypeS...]
    reshape x2 -> x0, local copies, waits for them, and re-layouts: 1.44 us -> none  [the longest x1 0.72 us: shards(): reach_back.reshape(blocks, BLOCK)]
    convert_element_type x1 -> x0, local copies, waits for them, and re-layouts: 0.76 us -> none  [shards(): reach = reach.astype(jnp.float32).T]
    broadcast_in_dim x1 -> x0, local copies, waits for them, and re-layouts: 0.59 us -> none  [shards(): jnp.broadcast_to(live.reshape(1, 1), (8, 128))]
where the time goes in v3:
time: 49.5 us; the launch traced here: 49.1 us
  Pallas kernels  46.2 us (93%)
  local copies, waits for them, and re-layouts  2.26 us (5%)
  between operations  0.66 us (1%)
    pallas_call x1, Pallas kernels, shards(): pl.pallas_call(functools.partial(kernel, M, R), out_shape=jax.ShapeDtypeS...  46.2 us
    unnamed x1, local copies, waits for them, and re-layouts  2.26 us

profile of v3, /device:TPU:3, one launch (start us, length us, event | category | flops | bytes accessed | tf_op | source)
XLA Modules:
  0.0 49.1 jit_solution(16441620999414794171)
XLA Ops:
  0.7 46.2 %consensus.1 = f32[512,512]{1,0:T(8,128)} custom-call(bf16[4096,512]{1,0:T(8,128)(2,1)} %x_hbm.1, s32[32,128]{1,0:T(8,128)} %bitcast.3, s32[32,128]{1,0:T(8,128)} %bitcast.4, s32[1]{0:T(128)S(6)} %copy.7.live_ref, s32[32,128]{1,0:T(8,128)} %bitcast.5), custom_call_target="tpu_custom_call" | custom-call | tf_op jit(solution)/shard_map/consensus/pallas_call | solution.py:409
  46.9 2.3 %copy.8 = f32[512,512]{1,0:T(8,128)} copy(f32[512,512]{1,0:T(8,128)} %consensus.1) | data formatting | bytes 2097152

commit v4 on v3

--- a/solution.py
+++ b/solution.py
@@ -1,4 +1,5 @@
 import functools
+import math
 
 import jax
 import jax.numpy as jnp
@@ -14,6 +15,7 @@
 MESH = pl.DeviceIdType.MESH
 
 sharpness = 3.0
+rate = sharpness * math.log2(math.e)
 
 
 def remote(src, dst, send_sem, recv_sem, device):
@@ -35,7 +37,7 @@
     ahead_ref,
     live_ref,
     ids_ref,
-    out_ref,
+    own,
     raw,
     ext,
     cons,
@@ -44,7 +46,6 @@
     live_in,
     reach_t,
     slots,
-    own,
     edge_out,
     edge_in,
     pair_out,
@@ -207,12 +208,26 @@
         limit = jnp.where(
             key_pos < 0, low_live - rows, jnp.where(key_pos >= rows, high_live + rows, live)
         )
-        key = jnp.where(key_pos < limit, key_lane.astype(f32), f32(-1e6))
-        inside = (key >= query - back) & (key <= query + ahead)
-        keep = inside | (key_lane.astype(f32) == query)
-        weight = jnp.where(keep, jnp.exp(sharpness * (scores - 1.0)), f32(0.0))
-        total = jnp.sum(weight, axis=1, keepdims=True)
-        mixed = jnp.dot(weight.astype(jnp.bfloat16), keys, preferred_element_type=f32)
+        present = key_pos < limit
+        key = key_lane.astype(f32)
+        never = f32(1e6)
+        key_up = jnp.where(present, key, -never)
+        key_down = jnp.where(present, key, never)
+        low, high = query - back, query + ahead
+        parts = [slice(k * BLOCK, (k + 1) * BLOCK) for k in range(3)]
+        middle = (key_up[:, parts[1]] >= low) & (key_up[:, parts[1]] <= high)
+        keep = [
+            key_up[:, parts[0]] >= low,
+            middle | (key[:, parts[1]] == query),
+            key_down[:, parts[2]] <= high,
+        ]
+        weights = [
+            jnp.where(keep[k], jnp.exp2((scores[:, parts[k]] - 1.0) * rate), f32(0.0))
+            for k in range(3)
+        ]
+        total = jnp.sum(weights[0] + weights[1] + weights[2], axis=1, keepdims=True)
+        weight = jnp.concatenate([w.astype(jnp.bfloat16) for w in weights], axis=1)
+        mixed = jnp.dot(weight, keys, preferred_element_type=f32)
         cons[pl.ds(at, BLOCK), :] = (mixed * (1.0 / total)).astype(jnp.bfloat16)
 
     def inner(p, carry):
@@ -368,10 +383,6 @@
     def _():
         edge_arrival(1)
 
-    owned = own[...]
-    scale = jnp.sqrt(jnp.mean(owned * owned, axis=1, keepdims=True) + 1e-06)
-    out_ref[...] = owned * (1.0 / scale)
-
     @pl.when(has_next)
     def _():
         for copy in to_next:
@@ -393,6 +404,12 @@
             pair_copy(j, t).wait_send()
         for j in range(H - 1):
             cross_copy(j, t).wait_send()
+
+
+def scale_rows(sum_ref, out_ref):
+    owned = sum_ref[...]
+    scale = jnp.sqrt(jnp.mean(owned * owned, axis=1, keepdims=True) + 1e-06)
+    out_ref[...] = owned * (1.0 / scale)
 
 
 def shards(spectra, reach_back, reach_ahead, live, cluster_ids):
@@ -406,7 +423,7 @@
     half = jnp.bfloat16
     dma = pltpu.SemaphoreType.DMA
     vmem = pl.BlockSpec(memory_space=pltpu.VMEM)
-    return pl.pallas_call(
+    sums = pl.pallas_call(
         functools.partial(kernel, M, R),
         out_shape=jax.ShapeDtypeStruct((CL_DEV, dim), jnp.float32),
         in_specs=[
@@ -426,7 +443,6 @@
             pltpu.VMEM((2, 8, LANES), jnp.int32),
             pltpu.VMEM((LANES, LANES), jnp.float32),
             pltpu.VMEM((1, rows), jnp.int32),
-            pltpu.VMEM(piece, jnp.float32),
             pltpu.VMEM((R,) + piece, half),
             pltpu.VMEM((2,) + piece, half),
             pltpu.VMEM((H,) + piece, half),
@@ -454,6 +470,15 @@
         live,
         cluster_ids.reshape(lines, LANES),
     )
+    tile = pl.BlockSpec((TILE, dim), lambda i: (i, 0))
+    return pl.pallas_call(
+        scale_rows,
+        out_shape=jax.ShapeDtypeStruct((CL_DEV, dim), jnp.float32),
+        grid=(tiles,),
+        in_specs=[tile],
+        out_specs=tile,
+        name="scale_rows",
+    )(sums)
 
 
 def solution(mesh):

time: 49.5 us -> 46.9 us (0.947)
  local copies, waits for them, and re-layouts: 2.26 us -> 0 us
    pallas_call x1, Pallas kernels: 46.2 us -> 43.6 us  [shards(): pl.pallas_call(functools.partial(kernel, M, R), out_shape=jax.ShapeDtypeS...]
    unnamed x1 -> x0, local copies, waits for them, and re-layouts: 2.26 us -> none
    pallas_call x0 -> x1, Pallas kernels: none -> 2.17 us  [shards(): pl.pallas_call(scale_rows, out_shape=jax.ShapeDtypeStruct((CL_DEV, dim),...]
where the time goes in v4:
time: 46.9 us; the launch traced here: 46.5 us
  Pallas kernels  45.8 us (98%)
  between operations  0.66 us (1%)
    pallas_call x1, Pallas kernels, shards(): pl.pallas_call(functools.partial(kernel, M, R), out_shape=jax.ShapeDtypeS...  43.6 us
    pallas_call x1, Pallas kernels, shards(): pl.pallas_call(scale_rows, out_shape=jax.ShapeDtypeStruct((CL_DEV, dim),...  2.17 us

profile of v4, /device:TPU:3, one launch (start us, length us, event | category | flops | bytes accessed | tf_op | source)
XLA Modules:
  0.0 46.5 jit_solution(1017302958803241613)
XLA Ops:
  0.7 43.6 %consensus.1.sum_ref = f32[512,512]{1,0:T(8,128)} custom-call(bf16[4096,512]{1,0:T(8,128)(2,1)} %x_hbm.1, s32[32,128]{1,0:T(8,128)} %bitcast.3, s32[32,128]{1,0:T(8,128)} %bitcast.4, s32[1]{0:T(128)S(6)} %copy.6.live_ref, s32[32,128]{1,0:T(8,128)} %bitcast.5), custom_call_target="tpu_custom_call" | custom-call | tf_op jit(solution)/shard_map/consensus/pallas_call | solution.py:426
  44.3 2.2 %scale_rows.1 = f32[512,512]{1,0:T(8,128)} custom-call(f32[512,512]{1,0:T(8,128)} %consensus.1.sum_ref), custom_call_target="tpu_custom_call" | custom-call | tf_op jit(solution)/shard_map/scale_rows/pallas_call | solution.py:474

commit v5 on v4

--- a/solution.py
+++ b/solution.py
@@ -336,7 +336,7 @@
 
         each_tile(2 * ((h + j + 1) % H) + 1 - c, use)
 
-    edges(0, R // 2)
+    edges(0, 1)
     for j in range(H - 1):
         give(j)
 
@@ -347,7 +347,7 @@
             cross_copy(j, t).start()
 
         each_tile(2 * ((h + j + 1) % H) + c, forward)
-    edges(R // 2, R)
+    edges(1, R)
     give(H - 1)
 
     def hold(t, at, value):

time: 46.9 us -> 50 us (1.066)
  Pallas kernels: 45.8 us -> 49 us
    pallas_call x1, Pallas kernels: 43.6 us -> 46.8 us  [shards(): pl.pallas_call(functools.partial(kernel, M, R), out_shape=jax.ShapeDtypeS...]
where the time goes in v5:
time: 50 us; the launch traced here: 49.6 us
  Pallas kernels  49 us (98%)
  between operations  0.66 us (1%)
    pallas_call x1, Pallas kernels, shards(): pl.pallas_call(functools.partial(kernel, M, R), out_shape=jax.ShapeDtypeS...  46.8 us
    pallas_call x1, Pallas kernels, shards(): pl.pallas_call(scale_rows, out_shape=jax.ShapeDtypeStruct((CL_DEV, dim),...  2.17 us

profile of v5, /device:TPU:3, one launch (start us, length us, event | category | flops | bytes accessed | tf_op | source)
XLA Modules:
  0.0 49.6 jit_solution(11652061610343487148)
XLA Ops:
  0.7 46.8 %consensus.1.sum_ref = f32[512,512]{1,0:T(8,128)} custom-call(bf16[4096,512]{1,0:T(8,128)(2,1)} %x_hbm.1, s32[32,128]{1,0:T(8,128)} %bitcast.3, s32[32,128]{1,0:T(8,128)} %bitcast.4, s32[1]{0:T(128)S(6)} %copy.6.live_ref, s32[32,128]{1,0:T(8,128)} %bitcast.5), custom_call_target="tpu_custom_call" | custom-call | tf_op jit(solution)/shard_map/consensus/pallas_call | solution.py:426
  47.5 2.2 %scale_rows.1 = f32[512,512]{1,0:T(8,128)} custom-call(f32[512,512]{1,0:T(8,128)} %consensus.1.sum_ref), custom_call_target="tpu_custom_call" | custom-call | tf_op jit(solution)/shard_map/scale_rows/pallas_call | solution.py:474
